TPU v7x, 32 devices: a whole 2x2x4 slice. The times are simulated.
32 devices in a mesh: grp: 8 (over y, x, core), seq: 4 (over z).
Axes of the slice: x: 2, y: 2, z: 4, core: 2. Of those that a mesh axis runs over, the one named last changes fastest.
Arguments:
- tokens: bfloat16 [8192, 2048], P(('grp', 'seq')), may hold values from -6 to 6
- cotangent: bfloat16 [8192, 2048], P(('grp', 'seq')), may hold values from -6 to 6
- segment_ids: int32 [8192], P(('grp', 'seq')), may hold values from 0 to 31, never falling along the last dimension, each value on 1 to 768 neighbouring positions
- tile_owner_slots: int32 [166], replicated, may hold values from 0 to 167, as said below
- weights_low: bfloat16 [168, 2048, 128], P('grp', 'seq')
- master: float32 [168, 2048, 128], P('grp', 'seq')
- moment_one: float32 [168, 2048, 128], P('grp', 'seq')
- moment_two: float32 [168, 2048, 128], P('grp', 'seq'), as said below
- left_basis_set: float32 [168, 2048, 512], P('grp', 'seq'), as said below
- right_basis_set: float32 [168, 512, 128], P('grp', 'seq'), as said below
- gains: float32 [2, 2048], replicated, may hold values from 0.5 to 1.5
- gain_moment_one: float32 [2, 2048], replicated, may hold values from -28 to 28
- gain_moment_two: float32 [2, 2048], replicated, may hold values from 430.8992 to 1720.32
Outputs:
- block_out: bfloat16 [8192, 2048], P(('grp', 'seq'))
- input_grad: float32 [8192, 2048], P(('grp', 'seq'))
- new_master: float32 [168, 2048, 128], P('grp', 'seq')
- new_moment_one: float32 [168, 2048, 128], P('grp', 'seq')
- new_moment_two: float32 [168, 2048, 128], P('grp', 'seq')
- gain_grads: float32 [2, 2048], replicated
- new_gains: float32 [2, 2048], replicated
- new_gain_one: float32 [2, 2048], replicated
- new_gain_two: float32 [2, 2048], replicated
Inputs may be any that keep to these rules, and one draw needn't show every extreme that they name: `tile_owner_slots`: the entries are distinct; slot q belongs to data group q // 21. `segment_ids`: never falls along the tokens. `left_basis_set`: each 512 x 512 block is orthogonal. `right_basis_set`: each 128 x 128 block is orthogonal. `moment_two`: positive.
All inputs are finite; a program needn't handle non-finite values.
Results may differ from a plain program's by a relative error of at most 0.015.
Values may be sent and summed in bfloat16 or wider, within the bound.
A program may use at most 704 MiB of HBM per device.

v0:
```python
import jax
import jax.numpy as jnp
from jax import lax
from jax.sharding import PartitionSpec as P

MODEL_WIDTH = 2048
NH = 16
HD = 128
FF = 5632
SEQLEN = 1024
NORM_EPS = 1e-05
BETA_ONE = 0.95
BETA_TWO = 0.95
ADAM_EPS = 1e-08
WEIGHT_DECAY = 0.01
LEARN_RATE = 0.03
GAIN_RATE = 1.5
ROPE_BASE = 10000.0
MASKED = -1e30
PRECISE = lax.Precision.HIGHEST


def rotate(values, positions, direction):
    head_width = values.shape[-1]
    half_width = head_width // 2
    frequency = ROPE_BASE ** (-(jnp.arange(half_width, dtype=jnp.float32) * 2.0) / head_width)
    angles = positions.astype(jnp.float32)[:, None] * frequency[None, :]
    cosine = jnp.cos(angles)[:, None, :]
    sine_part = (jnp.sin(angles) * direction)[:, None, :]
    leading = values[..., :half_width]
    trailing = values[..., half_width:]
    return jnp.concatenate(
        [leading * cosine - trailing * sine_part, trailing * cosine + leading * sine_part], axis=-1
    )


def visible(query_index, key_index, query_seg, key_seg):
    causal = query_index[:, None] >= key_index[None, :]
    same_seq = query_index[:, None] // SEQLEN == key_index[None, :] // SEQLEN
    same_doc = query_seg[:, None] == key_seg[None, :]
    return causal & same_seq & same_doc


def contract(left_side, right_side):
    return lax.dot_general(
        left_side, right_side, (((0,), (0,)), ((), ())), preferred_element_type=jnp.float32
    )


def times_transpose(left_side, right_side):
    return lax.dot_general(
        left_side, right_side, (((1,), (1,)), ((), ())), preferred_element_type=jnp.float32
    )


def attend(queries, key_rows, value_rows, query_index, query_seg, key_index, key_seg):
    query_total, head_count, head_width = queries.shape
    block_rows = min(512, query_total)
    block_count = query_total // block_rows
    score_scale = head_width ** (-0.5)

    def one_block(inputs):
        block_queries, block_index, block_seg = inputs
        raw_scores = jnp.einsum(
            "qhd,kd->hqk", block_queries, key_rows, preferred_element_type=jnp.float32
        )
        allowed = visible(block_index, key_index, block_seg, key_seg)
        score_matrix = jnp.where(allowed[None], raw_scores * score_scale, MASKED)
        highest = jnp.max(score_matrix, axis=-1, keepdims=True)
        exponent = jnp.exp(score_matrix - highest)
        totals = jnp.sum(exponent, axis=-1, keepdims=True)
        probs_low = (exponent / totals).astype(jnp.bfloat16)
        context = jnp.einsum(
            "hqk,kd->qhd", probs_low, value_rows, preferred_element_type=jnp.float32
        )
        return (context, jnp.transpose((highest + jnp.log(totals))[..., 0]))

    context, log_totals = lax.map(
        one_block,
        (
            queries.reshape(block_count, block_rows, head_count, head_width),
            query_index.reshape(block_count, block_rows),
            query_seg.reshape(block_count, block_rows),
        ),
    )
    return (
        context.reshape(query_total, head_count, head_width),
        log_totals.reshape(query_total, head_count),
    )


def attend_back(
    queries, key_rows, value_rows, grads_low, log_totals, query_index, query_seg, key_index, key_seg
):
    query_total, head_count, head_width = queries.shape
    block_rows = min(512, query_total)
    block_count = query_total // block_rows
    score_scale = head_width ** (-0.5)

    def one_block(running, inputs):
        block_queries, block_grads, block_totals, block_index, block_seg = inputs
        raw_scores = jnp.einsum(
            "qhd,kd->hqk", block_queries, key_rows, preferred_element_type=jnp.float32
        )
        allowed = visible(block_index, key_index, block_seg, key_seg)
        shifted = raw_scores * score_scale - jnp.transpose(block_totals)[:, :, None]
        probs = jnp.where(allowed[None], jnp.exp(shifted), 0.0)
        prob_grad = jnp.einsum(
            "qhd,kd->hqk", block_grads, value_rows, preferred_element_type=jnp.float32
        )
        centre = jnp.sum(probs * prob_grad, axis=-1, keepdims=True)
        score_grad = (probs * (prob_grad - centre) * score_scale).astype(jnp.bfloat16)
        query_part = jnp.einsum(
            "hqk,kd->qhd", score_grad, key_rows, preferred_element_type=jnp.float32
        )
        key_part = running[0] + jnp.einsum(
            "hqk,qhd->kd", score_grad, block_queries, preferred_element_type=jnp.float32
        )
        value_part = running[1] + jnp.einsum(
            "hqk,qhd->kd",
            probs.astype(jnp.bfloat16),
            block_grads,
            preferred_element_type=jnp.float32,
        )
        return ((key_part, value_part), query_part)

    zeros_rows = jnp.zeros(key_rows.shape, jnp.float32)
    (key_grad, value_grad), query_grad = lax.scan(
        one_block,
        (zeros_rows, zeros_rows),
        (
            queries.reshape(block_count, block_rows, head_count, head_width),
            grads_low.reshape(block_count, block_rows, head_count, head_width),
            log_totals.reshape(block_count, block_rows, head_count),
            query_index.reshape(block_count, block_rows),
            query_seg.reshape(block_count, block_rows),
        ),
    )
    return (query_grad.reshape(query_total, head_count, head_width), key_grad, value_grad)


def local(
    tokens,
    cotangent,
    segment_ids,
    tile_owner_slots,
    weights_low,
    master,
    moment_one,
    moment_two,
    left_basis_set,
    right_basis_set,
    gains,
    gain_moment_one,
    gain_moment_two,
):
    grp_count = lax.axis_size("grp")
    seq_count = lax.axis_size("seq")
    grp_here = lax.axis_index("grp")
    rows_here = tokens.shape[0]
    slots_here, rows_block, tile_width = weights_low.shape
    query_cols = NH * HD
    value_end = query_cols + 2 * HD
    output_end = value_end + MODEL_WIDTH
    attn_tiles = output_end // tile_width
    hidden_tiles = FF // tile_width
    share = -(-hidden_tiles // grp_count)
    share_cols = share * tile_width
    sub_rows = rows_block // grp_count
    local_index = lax.axis_index("seq") * rows_here + jnp.arange(rows_here, dtype=jnp.int32)
    local_place = local_index % SEQLEN
    plane_tiles = lax.all_gather(weights_low, "grp", axis=0, tiled=True)
    hidden_ids = grp_here * share + jnp.arange(share, dtype=jnp.int32)
    real = hidden_ids < hidden_tiles
    hidden_ids = jnp.minimum(hidden_ids, hidden_tiles - 1)
    feed_ids = (
        attn_tiles + jnp.arange(3, dtype=jnp.int32)[:, None] * hidden_tiles + hidden_ids[None, :]
    ).reshape(-1)
    attn_rows = lax.dynamic_slice_in_dim(plane_tiles, grp_here * sub_rows, sub_rows, axis=1)
    attn_rows = jnp.transpose(attn_rows[tile_owner_slots[:attn_tiles]], (1, 0, 2)).reshape(
        sub_rows, output_end
    )
    attn_weights = lax.all_gather(attn_rows, "seq", axis=0, tiled=False)
    attn_weights = lax.all_gather(attn_weights, "grp", axis=1, tiled=True).reshape(
        MODEL_WIDTH, output_end
    )
    feed_tiles = jnp.where(
        jnp.tile(real, 3)[:, None, None], plane_tiles[tile_owner_slots[feed_ids]], 0
    )
    feed_rows = jnp.transpose(feed_tiles, (1, 0, 2)).reshape(rows_block, 3 * share_cols)
    feed_weights = lax.all_gather(feed_rows, "seq", axis=0, tiled=True)
    cot_plane = lax.all_gather(cotangent, "grp", axis=0, tiled=True)
    tok_float = tokens.astype(jnp.float32)
    inverse_one = lax.rsqrt(jnp.mean(tok_float * tok_float, axis=-1, keepdims=True) + NORM_EPS)
    normed = (tok_float * inverse_one * gains[0]).astype(jnp.bfloat16)
    projected = jnp.dot(normed, attn_weights[:, :value_end], preferred_element_type=jnp.float32)
    queries = rotate(projected[:, :query_cols].reshape(rows_here, NH, HD), local_place, 1.0).astype(
        jnp.bfloat16
    )
    key_rows = (
        rotate(
            projected[:, query_cols : query_cols + HD].reshape(rows_here, 1, HD), local_place, 1.0
        )
        .reshape(rows_here, HD)
        .astype(jnp.bfloat16)
    )
    value_rows = projected[:, query_cols + HD : value_end].astype(jnp.bfloat16)
    all_pairs = lax.all_gather(
        jnp.concatenate([key_rows, value_rows], axis=1), "seq", axis=0, tiled=True
    )
    all_keys = all_pairs[:, :HD]
    all_values = all_pairs[:, HD:]
    all_segs = lax.all_gather(segment_ids, "seq", axis=0, tiled=True)
    group_index = jnp.arange(all_keys.shape[0], dtype=jnp.int32)
    group_place = group_index % SEQLEN
    heads_here = NH // seq_count
    head_queries = lax.all_to_all(
        queries.reshape(rows_here, query_cols), "seq", split_axis=1, concat_axis=0, tiled=True
    ).reshape(-1, heads_here, HD)
    head_context, log_totals = attend(
        head_queries, all_keys, all_values, group_index, all_segs, group_index, all_segs
    )
    context = lax.all_to_all(
        head_context.reshape(-1, heads_here * HD).astype(jnp.bfloat16),
        "seq",
        split_axis=0,
        concat_axis=1,
        tiled=True,
    )
    branch = jnp.dot(context, attn_weights[:, value_end:], preferred_element_type=jnp.float32)
    hidden = tok_float + branch
    inverse_two = lax.rsqrt(jnp.mean(hidden * hidden, axis=-1, keepdims=True) + NORM_EPS)
    normed_two = (hidden * inverse_two * gains[1]).astype(jnp.bfloat16)
    normed_plane = lax.all_gather(normed_two, "grp", axis=0, tiled=True)
    gating_weights = feed_weights[:, : 2 * share_cols]
    down_weights = feed_weights[:, 2 * share_cols :]
    gate_up = jnp.dot(normed_plane, gating_weights, preferred_element_type=jnp.float32)
    gate = gate_up[:, :share_cols]
    upper = gate_up[:, share_cols:]
    sigmoid_gate = jax.nn.sigmoid(gate)
    silu_gate = jax.nn.silu(gate)
    activated = (silu_gate * upper).astype(jnp.bfloat16)
    act_grad = jnp.dot(cot_plane, down_weights, preferred_element_type=jnp.float32)
    gate_grad = (act_grad * upper * sigmoid_gate * (1.0 + gate * (1.0 - sigmoid_gate))).astype(
        jnp.bfloat16
    )
    up_grad = (act_grad * silu_gate).astype(jnp.bfloat16)
    gating_grad = jnp.concatenate([gate_grad, up_grad], axis=1)
    norm_two_grad = lax.psum_scatter(
        times_transpose(gating_grad, gating_weights).astype(jnp.bfloat16),
        "grp",
        scatter_dimension=0,
        tiled=True,
    ).astype(jnp.float32)
    feed_grads = jnp.concatenate(
        [contract(normed_plane, gating_grad), contract(cot_plane, activated)], axis=1
    ).astype(jnp.bfloat16)
    feed_grads = lax.psum_scatter(feed_grads, "seq", scatter_dimension=0, tiled=True)
    feed_grads = jnp.transpose(feed_grads.reshape(rows_block, 3 * share, tile_width), (1, 0, 2))
    feed_grads = lax.all_gather(feed_grads, "grp", axis=0, tiled=True)
    feed_out = lax.psum_scatter(
        times_transpose(activated, down_weights).astype(jnp.bfloat16),
        "grp",
        scatter_dimension=0,
        tiled=True,
    ).astype(jnp.float32)
    block_out = (hidden + feed_out).astype(jnp.bfloat16)
    out_grad = cotangent.astype(jnp.float32)
    gain_two_term = jnp.sum(norm_two_grad * hidden * inverse_two, axis=0)
    hidden_grad = (
        out_grad
        + inverse_two * gains[1] * norm_two_grad
        - hidden
        * inverse_two**3
        * jnp.mean(hidden * gains[1] * norm_two_grad, axis=-1, keepdims=True)
    )
    branch_grad = hidden_grad.astype(jnp.bfloat16)
    context_grad = times_transpose(branch_grad, attn_weights[:, value_end:]).astype(jnp.bfloat16)
    head_grads = lax.all_to_all(
        context_grad, "seq", split_axis=1, concat_axis=0, tiled=True
    ).reshape(-1, heads_here, HD)

    def reduce_rows(part):
        cols = part.shape[1]
        blocks = jnp.transpose(
            part.astype(jnp.bfloat16).reshape(seq_count, grp_count, sub_rows, cols), (1, 0, 2, 3)
        ).reshape(grp_count * seq_count * sub_rows, cols)
        summed = lax.psum_scatter(blocks, ("grp", "seq"), scatter_dimension=0, tiled=True)
        return lax.all_gather(summed, "grp", axis=0, tiled=True)

    out_grads = reduce_rows(contract(context, branch_grad))
    head_query_grad, key_part, value_part = attend_back(
        head_queries,
        all_keys,
        all_values,
        head_grads,
        log_totals,
        group_index,
        all_segs,
        group_index,
        all_segs,
    )
    turned_query = (
        rotate(head_query_grad, group_place, -1.0).reshape(-1, heads_here * HD).astype(jnp.bfloat16)
    )
    query_grad = lax.all_to_all(turned_query, "seq", split_axis=0, concat_axis=1, tiled=True)
    key_part = rotate(key_part[:, None, :], group_place, -1.0)[:, 0, :]
    pair_grad = lax.psum_scatter(
        jnp.concatenate([key_part, value_part], axis=1), "seq", scatter_dimension=0, tiled=True
    )
    projected_grad = jnp.concatenate([query_grad, pair_grad.astype(jnp.bfloat16)], axis=1)
    in_grads = reduce_rows(contract(normed, projected_grad))
    norm_one_grad = times_transpose(projected_grad, attn_weights[:, :value_end])
    gain_one_term = jnp.sum(norm_one_grad * tok_float * inverse_one, axis=0)
    input_grad = (
        hidden_grad
        + inverse_one * gains[0] * norm_one_grad
        - tok_float
        * inverse_one**3
        * jnp.mean(tok_float * gains[0] * norm_one_grad, axis=-1, keepdims=True)
    )
    gain_grads = lax.psum(jnp.stack([gain_one_term, gain_two_term]), ("grp", "seq"))
    tile_count = tile_owner_slots.shape[0]
    tile_of_slot = (
        jnp.full((grp_count * slots_here,), tile_count, jnp.int32)
        .at[tile_owner_slots]
        .set(jnp.arange(tile_count, dtype=jnp.int32))
    )
    tiles_here = lax.dynamic_slice_in_dim(tile_of_slot, grp_here * slots_here, slots_here)
    attn_grads = jnp.transpose(
        jnp.concatenate([in_grads, out_grads], axis=1).reshape(rows_block, attn_tiles, tile_width),
        (1, 0, 2),
    )
    feed_at = jnp.clip(tiles_here - attn_tiles, 0, 3 * hidden_tiles - 1)
    which, column = (feed_at // hidden_tiles, feed_at % hidden_tiles)
    feed_at = column // share * (3 * share) + which * share + column % share
    picked = jnp.where(
        (tiles_here < attn_tiles)[:, None, None],
        attn_grads[jnp.minimum(tiles_here, attn_tiles - 1)],
        feed_grads[feed_at],
    )
    reduced_sum = jnp.where((tiles_here < tile_count)[:, None, None], picked, 0).astype(jnp.float32)
    turned = jnp.einsum("zji,zjc->zic", left_basis_set, reduced_sum)
    turned = jnp.einsum("zic,zcd->zid", turned, right_basis_set)
    new_one = BETA_ONE * moment_one + (1.0 - BETA_ONE) * turned
    new_two = BETA_TWO * moment_two + (1.0 - BETA_TWO) * turned * turned
    scaled = new_one / (jnp.sqrt(new_two) + ADAM_EPS)
    restored = jnp.einsum("zij,zjd->zid", left_basis_set, scaled)
    restored = jnp.einsum("zid,zed->zie", restored, right_basis_set)
    new_master = master * (1.0 - LEARN_RATE * WEIGHT_DECAY) - LEARN_RATE * restored
    gain_one = BETA_ONE * gain_moment_one + (1.0 - BETA_ONE) * gain_grads
    gain_two = BETA_TWO * gain_moment_two + (1.0 - BETA_TWO) * gain_grads * gain_grads
    new_gains = gains - GAIN_RATE * gain_one / (jnp.sqrt(gain_two) + ADAM_EPS)
    return (
        block_out,
        input_grad,
        new_master,
        new_one,
        new_two,
        gain_grads,
        new_gains,
        gain_one,
        gain_two,
    )


def solution(mesh):
    return jax.shard_map(
        local,
        mesh=mesh,
        in_specs=(
            P(("grp", "seq"), None),
            P(("grp", "seq"), None),
            P(("grp", "seq")),
            P(),
            P("grp", "seq", None),
            P("grp", "seq", None),
            P("grp", "seq", None),
            P("grp", "seq", None),
            P("grp", "seq", None),
            P("grp", "seq", None),
            P(),
            P(),
            P(),
        ),
        out_specs=(
            P(("grp", "seq"), None),
            P(("grp", "seq"), None),
            P("grp", "seq", None),
            P("grp", "seq", None),
            P("grp", "seq", None),
            P(),
            P(),
            P(),
            P(),
        ),
        check_vma=False,
    )
```

profile of v0, /device:TPU:0, one launch (start us, length us, event | category | flops | bytes accessed | tf_op | source)
XLA Modules:
  0.0 1731.6 jit_solution(6610942294189539147)
XLA Ops:
  8.7 116.0 %all-gather.11.cloned.1.call-done = bf16[168,512,128]{2,1,0:T(8,128)(2,1)} async-done(((bf16[21,512,128]{2,1,0:T(8,128)(2,1)}), bf16[168,512,128]{2,1,0:T(8,128)(2,1)}) %all-gather.11.cloned.1.call-update) | async-done | bytes 22020112 | tf_op jit(solution)/shard_map/all_gather | solution.py:172
  124.7 3.9 constant_dynamic-slice_fusion.5
  128.6 3.2 gather_fusion
  134.4 48.4 %all-gather.13.cloned.1.call-done = bf16[4,64,4352]{2,1,0:T(8,128)(2,1)} async-done(((bf16[1,64,4352]{2,1,0:T(8,128)(2,1)}), bf16[4,64,4352]{2,1,0:T(8,128)(2,1)}) %all-gather.13.cloned.1.call-update) | async-done | bytes 2228240 | tf_op jit(solution)/shard_map/all_gather | solution.py:183
  184.3 10.7 gather_fusion.2
  194.9 3.5 select_bitcast_fusion
  198.4 4.3 copy.107
  204.3 73.6 %all-gather.15.cloned.1.call-done = bf16[4,512,4352]{2,1,0:T(8,128)(2,1)} async-done(((bf16[4,64,4352]{2,1,0:T(8,128)(2,1)}), bf16[4,512,4352]{2,1,0:T(8,128)(2,1)}) %all-gather.15.cloned.1.call-update) | async-done | bytes 17825808 | tf_op jit(solution)/shard_map/all_gather | solution.py:184
  277.9 6.3 fusion.83
  291.7 4.6 all-to-all-start
  296.3 40.8 %all-gather = s32[4,1,256]{2,1,0:T(1,128)S(1)} all-gather(s32[1,1,256]{2,1,0:T(1,128)} %bitcast.336), channel_id=1, replica_groups=mesh['grp'=8,'seq'=4] {'seq'}, dimensions={0}, use_global_device_ids=true | all-gather | bytes 5120 | tf_op jit(solution)/shard_map/all_gather | solution.py:213
  339.6 43.2 %all_gather.37 = bf16[1024,256]{0,1:T(8,128)(2,1)S(1)} all-gather(bf16[256,256]{0,1:T(8,128)(2,1)S(1)} %pad_maximum_fusion.11), channel_id=1, replica_groups=mesh['grp'=8,'seq'=4] {'seq'}, dimensions={0}, use_global_device_ids=true | all-gather | bytes 655360 | tf_op jit(solution)/shard_map/all_gather | solution.py:208
  388.0 17.3 while.36
  393.2 3.5 fusion.216
  401.8 3.5 fusion.216
  410.6 59.3 %all_to_all.61 = bf16[4,256,512]{2,1,0:T(8,128)(2,1)} all-to-all(bf16[4,256,512]{2,1,0:T(8,128)(2,1)} %convert_element_type.137), channel_id=1, replica_groups=mesh['grp'=8,'seq'=4] {'seq'}, dimensions={0} | all-to-all | bytes 2097152 | tf_op jit(solution)/shard_map/all_to_all | solution.py:223
  472.1 6.4 multiply_reduce_fusion
  481.9 18.0 %all-gather.19.cloned.1.call-done = bf16[2048,2304]{0,1:T(8,128)(2,1)} async-done(((bf16[512,2304]{0,1:T(8,128)(2,1)}), bf16[2048,2304]{0,1:T(8,128)(2,1)}) %all-gather.19.cloned.1.call-update) | async-done | bytes 9437200 | tf_op jit(solution)/shard_map/all_gather | solution.py:191
  499.8 54.9 %all-gather.17.cloned.1.call-done = bf16[2048,2048]{1,0:T(8,128)(2,1)} async-done(((bf16[256,2048]{1,0:T(8,128)(2,1)}), bf16[2048,2048]{1,0:T(8,128)(2,1)}) %all-gather.17.cloned.1.call-update) | async-done | bytes 8388624 | tf_op jit(solution)/shard_map/all_gather | solution.py:234
  554.8 19.0 %fusion.95 = f32[2048,1536]{0,1:T(8,128)} fusion(bf16[2048,2048]{1,0:T(8,128)(2,1)} %all-gather.17.cloned.1.call-done, bf16[2048,2304]{0,1:T(8,128)(2,1)} %all-gather.19.cloned.1.call-done), kind=kOutput, calls=%fused_computation.134 | convolution fusion | flops 12884901888 | bytes 27262976 | tf_op jit(solution)/shard_map/dot_general | solution.py:237
  573.7 37.2 %all-gather.21.cloned.1.call-done = bf16[2048,2048]{1,0:T(8,128)(2,1)} async-done(((bf16[256,2048]{1,0:T(8,128)(2,1)}), bf16[2048,2048]{1,0:T(8,128)(2,1)}) %all-gather.21.cloned.1.call-update) | async-done | bytes 8388624 | tf_op jit(solution)/shard_map/all_gather | solution.py:192
  610.9 16.7 fusion.91
  629.3 18.7 %convolution_convert_fusion.3 = bf16[2048,2048]{1,0:T(8,128)(2,1)} fusion(bf16[2048,2304]{0,1:T(8,128)(2,1)} %all-gather.19.cloned.1.call-done, bf16[2048,768]{0,1:T(8,128)(2,1)} %get-tuple-element.680, bf16[2048,768]{0,1:T(8,128)(2,1)S(1)} %get-tuple-element.679), kind=kOutput, calls=%fused_computation.117 | convolution fusion | flops 12901679104 | bytes 20971520 | tf_op jit(solution)/shard_map/dot_general | solution.py:51
  648.1 11.9 convolution_convert_fusion.4
  660.0 59.5 %reduce-scatter.9.cloned.1.call-done = bf16[256,2048]{1,0:T(8,128)(2,1)} async-done(((bf16[2048,2048]{1,0:T(8,128)(2,1)}), bf16[256,2048]{1,0:T(8,128)(2,1)}) %reduce-scatter.9.cloned.1.call-update) | async-done | bytes 1048592 | tf_op jit(solution)/shard_map/reduce_scatter | solution.py:249
  722.5 72.2 %reduce-scatter.7.cloned.1.call-done = bf16[256,2048]{1,0:T(8,128)(2,1)} async-done(((bf16[2048,2048]{1,0:T(8,128)(2,1)}), bf16[256,2048]{1,0:T(8,128)(2,1)}) %reduce-scatter.7.cloned.1.call-update) | async-done | bytes 1048592 | tf_op jit(solution)/shard_map/reduce_scatter | solution.py:261
  794.7 4.2 fusion.121
  798.9 6.5 fusion.114
  806.5 4.6 all-to-all-start.2
  811.1 25.8 %all-to-all-done.2 = bf16[256,4,512]{2,0,1:T(8,128)(2,1)} async-done(((bf16[256,4,512]{2,0,1:T(8,128)(2,1)}), bf16[256,4,512]{2,0,1:T(8,128)(2,1)}, u32[]{:S(2)}, u32[]{:S(2)}) %all-to-all-start.2) | async-done | bytes 1048608 | tf_op jit(solution)/shard_map/all_to_all | solution.py:279
  839.5 123.5 %while.37 = (s32[]{:T(128)}, f32[1024,128]{1,0:T(8,128)}, f32[1024,128]{1,0:T(8,128)}, f32[2,512,4,128]{3,1,0,2:T(8,128)}, s32[2,512]{1,0:T(2,128)S(1)}, /*index...) while((s32[]{:T(128)}, f32[1024,128]{1,0:T(8,128)}, ...), condition=%wide.region_11.12_spmd.clone.clone, body=%wide.region_9.11_spmd.clone.clone.sunk | while | flops 2742048256 | bytes 106783928 | solution.py:128
  841.1 4.6 fusion.224
  845.9 4.5 fusion.223
  850.3 22.8 %fusion.228 = f32[2,512,4,128]{3,1,0,2:T(8,128)} fusion(f32[2,512,4,128]{3,1,0,2:T(8,128)} %get-tuple-element.900, s32[]{:T(128)} %get-tuple-element.897, f32[512,4,1024]{2,0,1:T(8,128)} %fusion.223, f32[512,4,1024]{2,0,1:T(8,128)} %fusion.224, f32[4,512]{1,0:T(4,128)S(1)} %dynamic-slice_bitcast_fusion.2, pred[512,1024]{1,0:T(8,128)(4,1)} %fusion.225, ...), kind=kOutput, calls=%fused_computation.67.clone.1 | convolution fusion | flops 559942656 | bytes 35930624 | tf_op jit(solution)/shard_map/while/body/eval_jaxpr/hqk,kd->qhd/dot_general | solution.py:113
  873.1 21.3 %fusion.226 = f32[1024,128]{1,0:T(8,128)} fusion(f32[512,4,1024]{2,0,1:T(8,128)} %fusion.223, f32[512,4,1024]{2,0,1:T(8,128)} %fusion.224, f32[4,512]{1,0:T(4,128)S(1)} %dynamic-slice_bitcast_fusion.2, pred[512,1024]{1,0:T(8,128)(4,1)} %fusion.225, f32[1024,128]{1,0:T(8,128)} %get-tuple-element.898, ...), kind=kOutput, calls=%fused_computation.70.clone.1 | convolution fusion | flops 560204800 | bytes 36192768 | tf_op jit(solution)/shard_map/while/body/eval_jaxpr/hqk,qhd->kd/dot_general | solution.py:116
  894.4 6.7 fusion.227
  902.7 4.6 fusion.224
  907.5 4.5 fusion.223
  912.0 22.8 %fusion.228 = f32[2,512,4,128]{3,1,0,2:T(8,128)} fusion(f32[2,512,4,128]{3,1,0,2:T(8,128)} %get-tuple-element.900, s32[]{:T(128)} %get-tuple-element.897, f32[512,4,1024]{2,0,1:T(8,128)} %fusion.223, f32[512,4,1024]{2,0,1:T(8,128)} %fusion.224, f32[4,512]{1,0:T(4,128)S(1)} %dynamic-slice_bitcast_fusion.2, pred[512,1024]{1,0:T(8,128)(4,1)} %fusion.225, ...), kind=kOutput, calls=%fused_computation.67.clone.1 | convolution fusion | flops 559942656 | bytes 35930624 | tf_op jit(solution)/shard_map/while/body/eval_jaxpr/hqk,kd->qhd/dot_general | solution.py:113
  934.8 21.3 %fusion.226 = f32[1024,128]{1,0:T(8,128)} fusion(f32[512,4,1024]{2,0,1:T(8,128)} %fusion.223, f32[512,4,1024]{2,0,1:T(8,128)} %fusion.224, f32[4,512]{1,0:T(4,128)S(1)} %dynamic-slice_bitcast_fusion.2, pred[512,1024]{1,0:T(8,128)(4,1)} %fusion.225, f32[1024,128]{1,0:T(8,128)} %get-tuple-element.898, ...), kind=kOutput, calls=%fused_computation.70.clone.1 | convolution fusion | flops 560204800 | bytes 36192768 | tf_op jit(solution)/shard_map/while/body/eval_jaxpr/hqk,qhd->kd/dot_general | solution.py:116
  956.1 6.9 fusion.227
  977.2 41.2 %all_to_all.62 = bf16[4,256,512]{2,1,0:T(8,128)(2,1)} all-to-all(bf16[4,256,512]{2,1,0:T(8,128)(2,1)} %convert_element_type.151), channel_id=1, replica_groups=mesh['grp'=8,'seq'=4] {'seq'}, dimensions={0} | all-to-all | bytes 2097152 | tf_op jit(solution)/shard_map/all_to_all | solution.py:306
  1021.1 5.3 convolution_convert_fusion
  1026.4 8.3 copy.118
  1036.3 6.9 convolution_convert_fusion.2
  1043.1 8.7 copy.119
  1052.0 10.8 fusion.102
  1062.7 15.9 convolution_convert_fusion.1
  1078.6 11.5 pad_maximum_fusion
  1090.2 79.3 %reduce-scatter.13.cloned.1.call-done = bf16[64,2304]{1,0:T(8,128)(2,1)} async-done(((bf16[2048,2304]{1,0:T(8,128)(2,1)}), bf16[64,2304]{1,0:T(8,128)(2,1)}) %reduce-scatter.13.cloned.1.call-update) | async-done | bytes 294928 | tf_op jit(solution)/shard_map/reduce_scatter | solution.py:288
  1169.6 187.0 %reduce-scatter.15.cloned.1.call-done = bf16[64,2048]{1,0:T(8,128)(2,1)} async-done(((bf16[2048,2048]{1,0:T(8,128)(2,1)}), bf16[64,2048]{1,0:T(8,128)(2,1)}) %reduce-scatter.15.cloned.1.call-update) | async-done | bytes 262160 | tf_op jit(solution)/shard_map/reduce_scatter | solution.py:288
  1356.7 161.1 %reduce-scatter.17.cloned.1.call-done = bf16[512,2304]{0,1:T(8,128)(2,1)} async-done(((bf16[2048,2304]{0,1:T(8,128)(2,1)}), bf16[512,2304]{0,1:T(8,128)(2,1)}) %reduce-scatter.17.cloned.1.call-update) | async-done | bytes 2359312 | tf_op jit(solution)/shard_map/reduce_scatter | solution.py:258
  1517.8 4.3 copy.122
  1525.1 9.3 fusion.133
  1534.5 41.6 %psum.7 = f32[2,2048]{1,0:T(2,128)S(1)} all-reduce(f32[2,2048]{1,0:T(2,128)S(1)} %pad_maximum_fusion.12), channel_id=1, replica_groups=mesh['grp'=8,'seq'=4] {'grp','seq'}, use_global_device_ids=true, to_apply=%region_20.21 | all-reduce | flops 4096 | bytes 32768 | tf_op jit(solution)/shard_map/psum | solution.py:322
  1578.1 3.9 fusion.129
  1582.0 4.7 pad_maximum_fusion.2
  1586.7 6.7 copy.120
  1593.4 6.7 copy.121
  1600.1 5.0 gather_fusion.3
  1605.0 76.1 %all-gather.27.cloned.1.call-done = bf16[144,512,128]{2,1,0:T(8,128)(2,1)} async-done(((bf16[18,512,128]{2,1,0:T(8,128)(2,1)}), bf16[144,512,128]{2,1,0:T(8,128)(2,1)}) %all-gather.27.cloned.1.call-update) | async-done | bytes 18874384 | tf_op jit(solution)/shard_map/all_gather | solution.py:260
  1681.1 8.9 gather_fusion.4
  1690.0 18.5 %fusion.97 = (f32[21,512,128]{2,1,0:T(8,128)}, f32[21,512,128]{2,1,0:T(8,128)}) fusion(f32[21,512,128]{2,1,0:T(8,128)} %param.24, f32[21,512,128]{2,1,0:T(8,128)} %param.23, f32[21,128,128]{2,1,0:T(8,128)S(1)} %copy-done, f32[21,512,512]{2,1,0:T(8,128)} %param.25, bf16[21,512,128]{2,1,0:T(8,128)(2,1)} %gather_fusion.3, ...), kind=kOutput, calls=%fused_computation.136 | convolution fusion | flops 1772617728 | bytes 50921512 | tf_op jit(solution)/shard_map/zic,zcd->zid/dot_general | solution.py:344
  1708.5 16.1 multiply_subtract_fusion
  (203 shorter events, 78.6 us)
Async XLA Ops:
  7.2 1682.9 %copy-start = (f32[21,128,128]{2,1,0:T(8,128)S(1)}, f32[21,128,128]{2,1,0:T(8,128)}, u32[]{:S(2)}) copy-start(f32[21,128,128]{2,1,0:T(8,128)} %param.26) | copy-start | bytes 4128772
  7.2 117.5 %all-gather.11.cloned.1.call-start = ((), (), s32[]{:S(2)}) async-start(), calls=%async_computation.10 | async-start | bytes 24772608 | tf_op jit(solution)/shard_map/all_gather | solution.py:172
  7.9 174.9 %all-gather.13.cloned.1.call-start = ((), (), s32[]{:S(2)}) async-start(), calls=%async_computation.11 | async-start | bytes 2785280 | tf_op jit(solution)/shard_map/all_gather | solution.py:183
  8.7 174.4 %copy-start.1 = (s32[166]{0:T(256)S(1)}, s32[166]{0:T(256)}, u32[]{:S(2)}) copy-start(s32[166]{0:T(256)} %param.20) | copy-start | bytes 1996
  8.7 175.3 %copy-start.7 = (bf16[256,2048]{1,0:T(8,128)(2,1)S(1)}, bf16[256,2048]{1,0:T(8,128)(2,1)}, u32[]{:S(2)}) copy-start(bf16[256,2048]{1,0:T(8,128)(2,1)} %param.17) | copy-start | bytes 3145732
  134.4 143.5 %all-gather.15.cloned.1.call-start = ((), (), s32[]{:S(2)}) async-start(), calls=%async_computation.12 | async-start | bytes 20054016 | tf_op jit(solution)/shard_map/all_gather | solution.py:184
  182.9 317.0 %all-gather.19.cloned.1.call-start = ((), (), s32[]{:S(2)}) async-start(), calls=%async_computation.14 | async-start | bytes 11796480 | tf_op jit(solution)/shard_map/all_gather | solution.py:191
  194.9 9.3 copy-start.15
  202.7 136.5 %copy-start.22 = (f32[64]{0:T(128)}, f32[64]{0:T(128)S(1)}, u32[]{:S(2)}) copy-start(f32[64]{0:T(128)S(1)} %multiply_power_fusion) | copy-start | bytes 772
  203.3 80.9 %copy-start.19 = (f32[256]{0:T(256)}, f32[256]{0:T(256)S(1)}, u32[]{:S(2)}) copy-start(f32[256]{0:T(256)S(1)} %get-tuple-element.703) | copy-start | bytes 3076
  204.3 80.0 %copy-start.13 = (f32[1,2048]{1,0:T(1,128)}, f32[1,2048]{1,0:T(1,128)S(1)}, u32[]{:S(2)}) copy-start(f32[1,2048]{1,0:T(1,128)S(1)} %get-tuple-element.697) | copy-start | bytes 24580
  284.3 1.4 copy-start.11
  291.7 91.5 %all-to-all-start = ((bf16[256,4,512]{0,2,1:T(8,128)(2,1)}), bf16[256,4,512]{0,2,1:T(8,128)(2,1)S(1)}, u32[]{:S(2)}, u32[]{:S(2)}) async-start(bf16[256,4,512]{0,2,1:T(8,128)(2,1)} %bitcast.5), calls=%async_computation | async-start | bytes 2097152 | tf_op jit(solution)/shard_map/all_to_all | solution.py:217
  296.3 258.4 %all-gather.17.cloned.1.call-start = ((), (), s32[]{:S(2)}) async-start(), calls=%async_computation.13 | async-start | bytes 9437184 | tf_op jit(solution)/shard_map/all_gather | solution.py:234
  478.5 1.3 copy-start.5
  481.1 129.9 %all-gather.21.cloned.1.call-start = ((), (), s32[]{:S(2)}) async-start(), calls=%async_computation.16 | async-start | bytes 9437184 | tf_op jit(solution)/shard_map/all_gather | solution.py:192
  481.7 237.9 %reduce-scatter.9.cloned.1.call-start = ((), (), s32[]{:S(2)}) async-start(), calls=%async_computation.17 | async-start | bytes 9437184 | tf_op jit(solution)/shard_map/reduce_scatter | solution.py:249
  627.6 1.7 copy-start.26
  648.1 146.6 %reduce-scatter.7.cloned.1.call-start = ((), (), s32[]{:S(2)}) async-start(), calls=%async_computation.15 | async-start | bytes 9437184 | tf_op jit(solution)/shard_map/reduce_scatter | solution.py:261
  798.9 6.5 copy-start.3
  806.5 30.4 %all-to-all-start.2 = ((bf16[256,4,512]{2,0,1:T(8,128)(2,1)}), bf16[256,4,512]{2,0,1:T(8,128)(2,1)}, u32[]{:S(2)}, u32[]{:S(2)}) async-start(bf16[256,4,512]{2,0,1:T(8,128)(2,1)} %bitcast.312), calls=%async_computation.4 | async-start | bytes 2097152 | tf_op jit(solution)/shard_map/all_to_all | solution.py:279
  811.1 208.7 %reduce-scatter.11.cloned.1.call-start = ((), (), s32[]{:S(2)}) async-start(), calls=%async_computation.18 | async-start | bytes 1310720 | tf_op jit(solution)/shard_map/reduce_scatter | solution.py:308
  839.5 127.7 %copy-start.23 = (f32[64]{0:T(128)S(1)}, f32[64]{0:T(128)}, u32[]{:S(2)}) copy-start(f32[64]{0:T(128)} %copy-done.22) | copy-start | bytes 772
  839.5 6.1 copy-start.6
  901.2 6.1 copy-start.6
  963.0 10.7 copy-start.9
  971.8 197.8 %reduce-scatter.13.cloned.1.call-start = ((), (), s32[]{:S(2)}) async-start(), calls=%async_computation.19 | async-start | bytes 9732096 | tf_op jit(solution)/shard_map/reduce_scatter | solution.py:288
  974.5 46.6 %copy-start.8 = (bf16[256,2048]{1,0:T(8,128)(2,1)S(1)}, bf16[256,2048]{1,0:T(8,128)(2,1)}, u32[]{:S(2)}) copy-start(bf16[256,2048]{1,0:T(8,128)(2,1)} %param.17) | copy-start | bytes 3145732
  974.5 46.6 %copy-start.14 = (f32[1,2048]{1,0:T(1,128)S(1)}, f32[1,2048]{1,0:T(1,128)}, u32[]{:S(2)}) copy-start(f32[1,2048]{1,0:T(1,128)} %copy-done.13) | copy-start | bytes 24580
  974.5 46.6 %copy-start.20 = (f32[256]{0:T(256)S(1)}, f32[256]{0:T(256)}, u32[]{:S(2)}) copy-start(f32[256]{0:T(256)} %copy-done.19) | copy-start | bytes 3076
  1019.8 6.6 copy-start.10
  1021.0 5.4 copy-start.12
  1034.7 1.6 copy-start.4
  1034.7 321.9 %reduce-scatter.15.cloned.1.call-start = ((), (), s32[]{:S(2)}) async-start(), calls=%async_computation.21 | async-start | bytes 8650752 | tf_op jit(solution)/shard_map/reduce_scatter | solution.py:288
  1051.9 465.9 %reduce-scatter.17.cloned.1.call-start = ((), (), s32[]{:S(2)}) async-start(), calls=%async_computation.23 | async-start | bytes 11796480 | tf_op jit(solution)/shard_map/reduce_scatter | solution.py:258
  1051.9 10.8 copy-start.27
  1052.0 10.8 copy-start.28
  1090.1 432.0 %copy-start.2 = (s32[166]{0:T(256)S(1)}, s32[166]{0:T(256)}, u32[]{:S(2)}) copy-start(s32[166]{0:T(256)} %param.20) | copy-start | bytes 1996
  1090.2 491.9 %all-gather.23.cloned.1.call-start = ((), (), s32[]{:S(2)}) async-start(), calls=%async_computation.20 | async-start | bytes 2654208 | tf_op jit(solution)/shard_map/all_gather | solution.py:289
  1169.5 412.5 %all-gather.25.cloned.1.call-start = ((), (), s32[]{:S(2)}) async-start(), calls=%async_computation.22 | async-start | bytes 2359296 | tf_op jit(solution)/shard_map/all_gather | solution.py:289
  1356.6 324.5 %all-gather.27.cloned.1.call-start = ((), (), s32[]{:S(2)}) async-start(), calls=%async_computation.24 | async-start | bytes 21233664 | tf_op jit(solution)/shard_map/all_gather | solution.py:260
  1525.1 9.3 copy-start.18
  1525.1 51.6 %copy-start.16 = (f32[2,2048]{1,0:T(2,128)S(1)}, f32[2,2048]{1,0:T(2,128)}, u32[]{:S(2)}) copy-start(f32[2,2048]{1,0:T(2,128)} %param.27) | copy-start | bytes 49156
  1525.1 51.6 %copy-start.21 = (f32[2,2048]{1,0:T(2,128)S(1)}, f32[2,2048]{1,0:T(2,128)}, u32[]{:S(2)}) copy-start(f32[2,2048]{1,0:T(2,128)} %param.28) | copy-start | bytes 49156
  1576.1 10.7 copy-start.17
  1600.1 90.0 %copy-start.24 = (pred[21]{0:T(512)(128)(4,1)S(1)}, pred[21]{0:T(512)(128)(4,1)}, u32[]{:S(2)}) copy-start(pred[21]{0:T(512)(128)(4,1)} %get-tuple-element.671) | copy-start | bytes 67
  1600.1 90.0 %copy-start.25 = (pred[21]{0:T(512)(128)(4,1)S(1)}, pred[21]{0:T(512)(128)(4,1)}, u32[]{:S(2)}) copy-start(pred[21]{0:T(512)(128)(4,1)} %broadcast_compare_fusion) | copy-start | bytes 67
Sparse Core Ops, SparseCore 0:
  9.9 114.7 all-gather.10
  134.5 48.3 all-gather.12
  184.8 93.1 all-gather.14
  279.9 219.8 all-gather.18
  502.1 52.5 all-gather.16
  556.5 54.3 all-gather.20
  648.2 71.2 reduce-scatter.8
  723.4 71.2 reduce-scatter.6
  971.9 35.7 reduce-scatter.10
  1034.8 134.6 reduce-scatter.12
  1171.8 184.7 reduce-scatter.14
  1358.8 158.9 reduce-scatter.16
  1519.7 30.3 all-gather.22
  1551.9 28.3 all-gather.24
  1582.5 98.5 all-gather.26
where the time goes:
time: 1740 us; the launch traced here: 1730 us
  waiting for transfers between devices  1010 us (58%)
  matrix products  299 us (17%)
  blocking collectives  226 us (13%)
  local copies, waits for them, and re-layouts  112 us (6%)
  other arithmetic  59.6 us (3%)
    reduce_scatter x2, waiting for transfers between devices, reduce_rows(): lax.psum_scatter(blocks, ('grp', 'seq'), scatter_dimension=0, tiled=True)  266 us
    reduce_scatter x1, waiting for transfers between devices, local(): lax.psum_scatter(feed_grads, 'seq', scatter_dimension=0, tiled=True)  161 us
    all_gather x1, waiting for transfers between devices, local(): plane_tiles = lax.all_gather(weights_low, 'grp', axis=0, tiled=True)  116 us
    all_gather x1, waiting for transfers between devices, local(): feed_grads = lax.all_gather(feed_grads, 'grp', axis=0, tiled=True)  76.1 us
    all_gather x1, waiting for transfers between devices, local(): lax.all_gather(attn_weights, 'grp', axis=1, tiled=True)  73.6 us
    reduce_scatter x1, waiting for transfers between devices, local(): lax.psum_scatter(times_transpose(activated, down_weights).astype(jnp.bflo...  72.2 us
    reduce_scatter x1, waiting for transfers between devices, local(): lax.psum_scatter(times_transpose(gating_grad, gating_weights).astype(jnp....  59.5 us
    all_to_all x1, blocking collectives, local(): lax.all_to_all(head_context.reshape(-1, heads_here * HD).astype(jnp.bfloa...  59.3 us
  transfers between devices with their start and end apart: 17, of which 13 were waited for; matrix products, arithmetic and copies ran while one was open for 12% of the time, Pallas kernels for 0%

commit v1 on v0

--- a/solution.py
+++ b/solution.py
@@ -319,7 +319,7 @@
         * inverse_one**3
         * jnp.mean(tok_float * gains[0] * norm_one_grad, axis=-1, keepdims=True)
     )
-    gain_grads = lax.psum(jnp.stack([gain_one_term, gain_two_term]), ("grp", "seq"))
+    gain_grads = lax.psum(lax.psum(jnp.stack([gain_one_term, gain_two_term]), "seq"), "grp")
     tile_count = tile_owner_slots.shape[0]
     tile_of_slot = (
         jnp.full((grp_count * slots_here,), tile_count, jnp.int32)

time: 1740 us -> 1740 us (level)
    psum x1 -> x2, blocking collectives: 41.6 us -> 41.2 us  [the longest x1 23 us: local(): lax.psum(lax.psum(jnp.stack([gain_one_term, gain_two_term]), 'seq'), 'grp')]
where the time goes in v1:
time: 1740 us; the launch traced here: 1730 us
  waiting for transfers between devices  1010 us (58%)
  matrix products  299 us (17%)
  blocking collectives  226 us (13%)
  local copies, waits for them, and re-layouts  111 us (6%)
  other arithmetic  59.5 us (3%)
    reduce_scatter x2, waiting for transfers between devices, reduce_rows(): lax.psum_scatter(blocks, ('grp', 'seq'), scatter_dimension=0, tiled=True)  266 us
    reduce_scatter x1, waiting for transfers between devices, local(): lax.psum_scatter(feed_grads, 'seq', scatter_dimension=0, tiled=True)  161 us
    all_gather x1, waiting for transfers between devices, local(): plane_tiles = lax.all_gather(weights_low, 'grp', axis=0, tiled=True)  116 us
    all_gather x1, waiting for transfers between devices, local(): feed_grads = lax.all_gather(feed_grads, 'grp', axis=0, tiled=True)  75.8 us
    all_gather x1, waiting for transfers between devices, local(): lax.all_gather(attn_weights, 'grp', axis=1, tiled=True)  73.6 us
    reduce_scatter x1, waiting for transfers between devices, local(): lax.psum_scatter(times_transpose(activated, down_weights).astype(jnp.bflo...  72.2 us
    reduce_scatter x1, waiting for transfers between devices, local(): lax.psum_scatter(times_transpose(gating_grad, gating_weights).astype(jnp....  59.5 us
    all_to_all x1, blocking collectives, local(): lax.all_to_all(head_context.reshape(-1, heads_here * HD).astype(jnp.bfloa...  59.3 us
  transfers between devices with their start and end apart: 17, of which 13 were waited for; matrix products, arithmetic and copies ran while one was open for 12% of the time, Pallas kernels for 0%

profile of v1, /device:TPU:0, one launch (start us, length us, event | category | flops | bytes accessed | tf_op | source)
XLA Modules:
  0.0 1730.9 jit_solution(2232771411483398638)
XLA Ops:
  8.7 116.0 %all-gather.11.cloned.1.call-done = bf16[168,512,128]{2,1,0:T(8,128)(2,1)} async-done(((bf16[21,512,128]{2,1,0:T(8,128)(2,1)}), bf16[168,512,128]{2,1,0:T(8,128)(2,1)}) %all-gather.11.cloned.1.call-update) | async-done | bytes 22020112 | tf_op jit(solution)/shard_map/all_gather | solution.py:172
  124.7 3.9 constant_dynamic-slice_fusion.5
  134.4 48.4 %all-gather.13.cloned.1.call-done = bf16[4,64,4352]{2,1,0:T(8,128)(2,1)} async-done(((bf16[1,64,4352]{2,1,0:T(8,128)(2,1)}), bf16[4,64,4352]{2,1,0:T(8,128)(2,1)}) %all-gather.13.cloned.1.call-update) | async-done | bytes 2228240 | tf_op jit(solution)/shard_map/all_gather | solution.py:183
  184.3 10.7 gather_fusion.2
  194.9 3.5 select_bitcast_fusion
  198.4 4.3 copy.107
  204.3 73.6 %all-gather.15.cloned.1.call-done = bf16[4,512,4352]{2,1,0:T(8,128)(2,1)} async-done(((bf16[4,64,4352]{2,1,0:T(8,128)(2,1)}), bf16[4,512,4352]{2,1,0:T(8,128)(2,1)}) %all-gather.15.cloned.1.call-update) | async-done | bytes 17825808 | tf_op jit(solution)/shard_map/all_gather | solution.py:184
  277.9 6.3 fusion.83
  291.7 4.6 all-to-all-start
  296.3 40.8 %all-gather = s32[4,1,256]{2,1,0:T(1,128)S(1)} all-gather(s32[1,1,256]{2,1,0:T(1,128)} %bitcast.336), channel_id=1, replica_groups=mesh['grp'=8,'seq'=4] {'seq'}, dimensions={0}, use_global_device_ids=true | all-gather | bytes 5120 | tf_op jit(solution)/shard_map/all_gather | solution.py:213
  339.6 43.2 %all_gather.37 = bf16[1024,256]{0,1:T(8,128)(2,1)S(1)} all-gather(bf16[256,256]{0,1:T(8,128)(2,1)S(1)} %pad_maximum_fusion.11), channel_id=1, replica_groups=mesh['grp'=8,'seq'=4] {'seq'}, dimensions={0}, use_global_device_ids=true | all-gather | bytes 655360 | tf_op jit(solution)/shard_map/all_gather | solution.py:208
  388.0 17.3 while.36
  393.2 3.5 fusion.216
  401.8 3.5 fusion.216
  410.6 59.3 %all_to_all.61 = bf16[4,256,512]{2,1,0:T(8,128)(2,1)} all-to-all(bf16[4,256,512]{2,1,0:T(8,128)(2,1)} %convert_element_type.137), channel_id=1, replica_groups=mesh['grp'=8,'seq'=4] {'seq'}, dimensions={0} | all-to-all | bytes 2097152 | tf_op jit(solution)/shard_map/all_to_all | solution.py:223
  472.1 6.5 multiply_reduce_fusion
  482.0 17.8 %all-gather.19.cloned.1.call-done = bf16[2048,2304]{0,1:T(8,128)(2,1)} async-done(((bf16[512,2304]{0,1:T(8,128)(2,1)}), bf16[2048,2304]{0,1:T(8,128)(2,1)}) %all-gather.19.cloned.1.call-update) | async-done | bytes 9437200 | tf_op jit(solution)/shard_map/all_gather | solution.py:191
  499.8 54.9 %all-gather.17.cloned.1.call-done = bf16[2048,2048]{1,0:T(8,128)(2,1)} async-done(((bf16[256,2048]{1,0:T(8,128)(2,1)}), bf16[2048,2048]{1,0:T(8,128)(2,1)}) %all-gather.17.cloned.1.call-update) | async-done | bytes 8388624 | tf_op jit(solution)/shard_map/all_gather | solution.py:234
  554.8 19.1 %fusion.95 = f32[2048,1536]{0,1:T(8,128)} fusion(bf16[2048,2048]{1,0:T(8,128)(2,1)} %all-gather.17.cloned.1.call-done, bf16[2048,2304]{0,1:T(8,128)(2,1)} %all-gather.19.cloned.1.call-done), kind=kOutput, calls=%fused_computation.134 | convolution fusion | flops 12884901888 | bytes 27262976 | tf_op jit(solution)/shard_map/dot_general | solution.py:237
  573.8 37.1 %all-gather.21.cloned.1.call-done = bf16[2048,2048]{1,0:T(8,128)(2,1)} async-done(((bf16[256,2048]{1,0:T(8,128)(2,1)}), bf16[2048,2048]{1,0:T(8,128)(2,1)}) %all-gather.21.cloned.1.call-update) | async-done | bytes 8388624 | tf_op jit(solution)/shard_map/all_gather | solution.py:192
  610.9 16.7 fusion.91
  629.3 18.7 %convolution_convert_fusion.3 = bf16[2048,2048]{1,0:T(8,128)(2,1)} fusion(bf16[2048,2304]{0,1:T(8,128)(2,1)} %all-gather.19.cloned.1.call-done, bf16[2048,768]{0,1:T(8,128)(2,1)} %get-tuple-element.680, bf16[2048,768]{0,1:T(8,128)(2,1)S(1)} %get-tuple-element.679), kind=kOutput, calls=%fused_computation.117 | convolution fusion | flops 12901679104 | bytes 20971520 | tf_op jit(solution)/shard_map/dot_general | solution.py:51
  648.1 11.9 convolution_convert_fusion.4
  660.0 59.5 %reduce-scatter.9.cloned.1.call-done = bf16[256,2048]{1,0:T(8,128)(2,1)} async-done(((bf16[2048,2048]{1,0:T(8,128)(2,1)}), bf16[256,2048]{1,0:T(8,128)(2,1)}) %reduce-scatter.9.cloned.1.call-update) | async-done | bytes 1048592 | tf_op jit(solution)/shard_map/reduce_scatter | solution.py:249
  722.5 72.2 %reduce-scatter.7.cloned.1.call-done = bf16[256,2048]{1,0:T(8,128)(2,1)} async-done(((bf16[2048,2048]{1,0:T(8,128)(2,1)}), bf16[256,2048]{1,0:T(8,128)(2,1)}) %reduce-scatter.7.cloned.1.call-update) | async-done | bytes 1048592 | tf_op jit(solution)/shard_map/reduce_scatter | solution.py:261
  794.6 4.2 fusion.121
  798.9 6.5 fusion.114
  806.5 4.6 all-to-all-start.2
  811.1 25.8 %all-to-all-done.2 = bf16[256,4,512]{2,0,1:T(8,128)(2,1)} async-done(((bf16[256,4,512]{2,0,1:T(8,128)(2,1)}), bf16[256,4,512]{2,0,1:T(8,128)(2,1)}, u32[]{:S(2)}, u32[]{:S(2)}) %all-to-all-start.2) | async-done | bytes 1048608 | tf_op jit(solution)/shard_map/all_to_all | solution.py:279
  839.5 123.6 %while.37 = (s32[]{:T(128)}, f32[1024,128]{1,0:T(8,128)}, f32[1024,128]{1,0:T(8,128)}, f32[2,512,4,128]{3,1,0,2:T(8,128)}, s32[2,512]{1,0:T(2,128)S(1)}, /*index...) while((s32[]{:T(128)}, f32[1024,128]{1,0:T(8,128)}, ...), condition=%wide.region_11.12_spmd.clone.clone, body=%wide.region_9.11_spmd.clone.clone.sunk | while | flops 2742048256 | bytes 106783928 | solution.py:128
  841.1 4.6 fusion.224
  845.8 4.5 fusion.223
  850.3 22.9 %fusion.228 = f32[2,512,4,128]{3,1,0,2:T(8,128)} fusion(f32[2,512,4,128]{3,1,0,2:T(8,128)} %get-tuple-element.900, s32[]{:T(128)} %get-tuple-element.897, f32[512,4,1024]{2,0,1:T(8,128)} %fusion.223, f32[512,4,1024]{2,0,1:T(8,128)} %fusion.224, f32[4,512]{1,0:T(4,128)S(1)} %dynamic-slice_bitcast_fusion.2, pred[512,1024]{1,0:T(8,128)(4,1)} %fusion.225, ...), kind=kOutput, calls=%fused_computation.67.clone.1 | convolution fusion | flops 559942656 | bytes 35930624 | tf_op jit(solution)/shard_map/while/body/eval_jaxpr/hqk,kd->qhd/dot_general | solution.py:113
  873.2 21.2 %fusion.226 = f32[1024,128]{1,0:T(8,128)} fusion(f32[512,4,1024]{2,0,1:T(8,128)} %fusion.223, f32[512,4,1024]{2,0,1:T(8,128)} %fusion.224, f32[4,512]{1,0:T(4,128)S(1)} %dynamic-slice_bitcast_fusion.2, pred[512,1024]{1,0:T(8,128)(4,1)} %fusion.225, f32[1024,128]{1,0:T(8,128)} %get-tuple-element.898, ...), kind=kOutput, calls=%fused_computation.70.clone.1 | convolution fusion | flops 560204800 | bytes 36192768 | tf_op jit(solution)/shard_map/while/body/eval_jaxpr/hqk,qhd->kd/dot_general | solution.py:116
  894.4 6.7 fusion.227
  902.7 4.6 fusion.224
  907.5 4.5 fusion.223
  912.0 22.9 %fusion.228 = f32[2,512,4,128]{3,1,0,2:T(8,128)} fusion(f32[2,512,4,128]{3,1,0,2:T(8,128)} %get-tuple-element.900, s32[]{:T(128)} %get-tuple-element.897, f32[512,4,1024]{2,0,1:T(8,128)} %fusion.223, f32[512,4,1024]{2,0,1:T(8,128)} %fusion.224, f32[4,512]{1,0:T(4,128)S(1)} %dynamic-slice_bitcast_fusion.2, pred[512,1024]{1,0:T(8,128)(4,1)} %fusion.225, ...), kind=kOutput, calls=%fused_computation.67.clone.1 | convolution fusion | flops 559942656 | bytes 35930624 | tf_op jit(solution)/shard_map/while/body/eval_jaxpr/hqk,kd->qhd/dot_general | solution.py:113
  934.9 21.3 %fusion.226 = f32[1024,128]{1,0:T(8,128)} fusion(f32[512,4,1024]{2,0,1:T(8,128)} %fusion.223, f32[512,4,1024]{2,0,1:T(8,128)} %fusion.224, f32[4,512]{1,0:T(4,128)S(1)} %dynamic-slice_bitcast_fusion.2, pred[512,1024]{1,0:T(8,128)(4,1)} %fusion.225, f32[1024,128]{1,0:T(8,128)} %get-tuple-element.898, ...), kind=kOutput, calls=%fused_computation.70.clone.1 | convolution fusion | flops 560204800 | bytes 36192768 | tf_op jit(solution)/shard_map/while/body/eval_jaxpr/hqk,qhd->kd/dot_general | solution.py:116
  956.2 6.9 fusion.227
  977.2 41.2 %all_to_all.62 = bf16[4,256,512]{2,1,0:T(8,128)(2,1)} all-to-all(bf16[4,256,512]{2,1,0:T(8,128)(2,1)} %convert_element_type.151), channel_id=1, replica_groups=mesh['grp'=8,'seq'=4] {'seq'}, dimensions={0} | all-to-all | bytes 2097152 | tf_op jit(solution)/shard_map/all_to_all | solution.py:306
  1021.1 5.3 convolution_convert_fusion
  1026.4 8.3 copy.118
  1036.3 6.9 convolution_convert_fusion.2
  1043.1 8.7 copy.119
  1052.0 10.8 fusion.102
  1062.8 15.9 convolution_convert_fusion.1
  1078.6 11.5 pad_maximum_fusion
  1090.2 79.0 %reduce-scatter.13.cloned.1.call-done = bf16[64,2304]{1,0:T(8,128)(2,1)} async-done(((bf16[2048,2304]{1,0:T(8,128)(2,1)}), bf16[64,2304]{1,0:T(8,128)(2,1)}) %reduce-scatter.13.cloned.1.call-update) | async-done | bytes 294928 | tf_op jit(solution)/shard_map/reduce_scatter | solution.py:288
  1169.3 187.3 %reduce-scatter.15.cloned.1.call-done = bf16[64,2048]{1,0:T(8,128)(2,1)} async-done(((bf16[2048,2048]{1,0:T(8,128)(2,1)}), bf16[64,2048]{1,0:T(8,128)(2,1)}) %reduce-scatter.15.cloned.1.call-update) | async-done | bytes 262160 | tf_op jit(solution)/shard_map/reduce_scatter | solution.py:288
  1356.7 161.1 %reduce-scatter.17.cloned.1.call-done = bf16[512,2304]{0,1:T(8,128)(2,1)} async-done(((bf16[2048,2304]{0,1:T(8,128)(2,1)}), bf16[512,2304]{0,1:T(8,128)(2,1)}) %reduce-scatter.17.cloned.1.call-update) | async-done | bytes 2359312 | tf_op jit(solution)/shard_map/reduce_scatter | solution.py:258
  1517.8 4.3 copy.122
  1525.1 9.3 fusion.133
  1534.4 18.2 %psum.14 = f32[2,2048]{1,0:T(2,128)S(1)} all-reduce(f32[2,2048]{1,0:T(2,128)S(1)} %pad_maximum_fusion.12), channel_id=1, replica_groups=mesh['grp'=8,'seq'=4] {'seq'}, use_global_device_ids=true, to_apply=%region_20.21 | all-reduce | flops 4096 | bytes 32768 | tf_op jit(solution)/shard_map/psum | solution.py:322
  1552.6 23.0 %psum.15 = f32[2,2048]{1,0:T(2,128)S(1)} all-reduce(f32[2,2048]{1,0:T(2,128)S(1)} %psum.14), channel_id=1, replica_groups=mesh['grp'=8,'seq'=4] {'grp'}, use_global_device_ids=true, to_apply=%region_21.22 | all-reduce | flops 4096 | bytes 32768 | tf_op jit(solution)/shard_map/psum | solution.py:322
  1577.7 3.9 fusion.129
  1581.6 4.7 pad_maximum_fusion.2
  1586.3 6.7 copy.120
  1592.9 6.6 copy.121
  1599.6 4.9 gather_fusion.3
  1604.5 75.8 %all-gather.27.cloned.1.call-done = bf16[144,512,128]{2,1,0:T(8,128)(2,1)} async-done(((bf16[18,512,128]{2,1,0:T(8,128)(2,1)}), bf16[144,512,128]{2,1,0:T(8,128)(2,1)}) %all-gather.27.cloned.1.call-update) | async-done | bytes 18874384 | tf_op jit(solution)/shard_map/all_gather | solution.py:260
  1680.3 8.9 gather_fusion.4
  1689.3 18.5 %fusion.97 = (f32[21,512,128]{2,1,0:T(8,128)}, f32[21,512,128]{2,1,0:T(8,128)}) fusion(f32[21,512,128]{2,1,0:T(8,128)} %param.24, f32[21,512,128]{2,1,0:T(8,128)} %param.23, f32[21,128,128]{2,1,0:T(8,128)S(1)} %copy-done, f32[21,512,512]{2,1,0:T(8,128)} %param.25, bf16[21,512,128]{2,1,0:T(8,128)(2,1)} %gather_fusion.3, ...), kind=kOutput, calls=%fused_computation.136 | convolution fusion | flops 1772617728 | bytes 50921512 | tf_op jit(solution)/shard_map/zic,zcd->zid/dot_general | solution.py:344
  1707.8 16.1 multiply_subtract_fusion
  (204 shorter events, 81.8 us)
Async XLA Ops:
  7.2 1682.1 %copy-start = (f32[21,128,128]{2,1,0:T(8,128)S(1)}, f32[21,128,128]{2,1,0:T(8,128)}, u32[]{:S(2)}) copy-start(f32[21,128,128]{2,1,0:T(8,128)} %param.26) | copy-start | bytes 4128772
  7.2 117.5 %all-gather.11.cloned.1.call-start = ((), (), s32[]{:S(2)}) async-start(), calls=%async_computation.10 | async-start | bytes 24772608 | tf_op jit(solution)/shard_map/all_gather | solution.py:172
  7.9 174.9 %all-gather.13.cloned.1.call-start = ((), (), s32[]{:S(2)}) async-start(), calls=%async_computation.11 | async-start | bytes 2785280 | tf_op jit(solution)/shard_map/all_gather | solution.py:183
  8.7 174.4 %copy-start.1 = (s32[166]{0:T(256)S(1)}, s32[166]{0:T(256)}, u32[]{:S(2)}) copy-start(s32[166]{0:T(256)} %param.20) | copy-start | bytes 1996
  8.7 175.3 %copy-start.7 = (bf16[256,2048]{1,0:T(8,128)(2,1)S(1)}, bf16[256,2048]{1,0:T(8,128)(2,1)}, u32[]{:S(2)}) copy-start(bf16[256,2048]{1,0:T(8,128)(2,1)} %param.17) | copy-start | bytes 3145732
  134.4 143.5 %all-gather.15.cloned.1.call-start = ((), (), s32[]{:S(2)}) async-start(), calls=%async_computation.12 | async-start | bytes 20054016 | tf_op jit(solution)/shard_map/all_gather | solution.py:184
  182.9 317.0 %all-gather.19.cloned.1.call-start = ((), (), s32[]{:S(2)}) async-start(), calls=%async_computation.14 | async-start | bytes 11796480 | tf_op jit(solution)/shard_map/all_gather | solution.py:191
  194.9 9.3 copy-start.15
  202.7 136.5 %copy-start.22 = (f32[64]{0:T(128)}, f32[64]{0:T(128)S(1)}, u32[]{:S(2)}) copy-start(f32[64]{0:T(128)S(1)} %multiply_power_fusion) | copy-start | bytes 772
  203.3 80.9 %copy-start.19 = (f32[256]{0:T(256)}, f32[256]{0:T(256)S(1)}, u32[]{:S(2)}) copy-start(f32[256]{0:T(256)S(1)} %get-tuple-element.703) | copy-start | bytes 3076
  204.3 80.0 %copy-start.13 = (f32[1,2048]{1,0:T(1,128)}, f32[1,2048]{1,0:T(1,128)S(1)}, u32[]{:S(2)}) copy-start(f32[1,2048]{1,0:T(1,128)S(1)} %get-tuple-element.697) | copy-start | bytes 24580
  284.3 1.4 copy-start.11
  291.7 91.5 %all-to-all-start = ((bf16[256,4,512]{0,2,1:T(8,128)(2,1)}), bf16[256,4,512]{0,2,1:T(8,128)(2,1)S(1)}, u32[]{:S(2)}, u32[]{:S(2)}) async-start(bf16[256,4,512]{0,2,1:T(8,128)(2,1)} %bitcast.5), calls=%async_computation | async-start | bytes 2097152 | tf_op jit(solution)/shard_map/all_to_all | solution.py:217
  296.3 258.4 %all-gather.17.cloned.1.call-start = ((), (), s32[]{:S(2)}) async-start(), calls=%async_computation.13 | async-start | bytes 9437184 | tf_op jit(solution)/shard_map/all_gather | solution.py:234
  478.7 1.3 copy-start.5
  481.2 129.7 %all-gather.21.cloned.1.call-start = ((), (), s32[]{:S(2)}) async-start(), calls=%async_computation.16 | async-start | bytes 9437184 | tf_op jit(solution)/shard_map/all_gather | solution.py:192
  481.8 237.7 %reduce-scatter.9.cloned.1.call-start = ((), (), s32[]{:S(2)}) async-start(), calls=%async_computation.17 | async-start | bytes 9437184 | tf_op jit(solution)/shard_map/reduce_scatter | solution.py:249
  627.6 1.7 copy-start.26
  648.0 146.6 %reduce-scatter.7.cloned.1.call-start = ((), (), s32[]{:S(2)}) async-start(), calls=%async_computation.15 | async-start | bytes 9437184 | tf_op jit(solution)/shard_map/reduce_scatter | solution.py:261
  798.9 6.5 copy-start.3
  806.5 30.4 %all-to-all-start.2 = ((bf16[256,4,512]{2,0,1:T(8,128)(2,1)}), bf16[256,4,512]{2,0,1:T(8,128)(2,1)}, u32[]{:S(2)}, u32[]{:S(2)}) async-start(bf16[256,4,512]{2,0,1:T(8,128)(2,1)} %bitcast.312), calls=%async_computation.4 | async-start | bytes 2097152 | tf_op jit(solution)/shard_map/all_to_all | solution.py:279
  811.1 208.8 %reduce-scatter.11.cloned.1.call-start = ((), (), s32[]{:S(2)}) async-start(), calls=%async_computation.18 | async-start | bytes 1310720 | tf_op jit(solution)/shard_map/reduce_scatter | solution.py:308
  839.5 127.8 %copy-start.23 = (f32[64]{0:T(128)S(1)}, f32[64]{0:T(128)}, u32[]{:S(2)}) copy-start(f32[64]{0:T(128)} %copy-done.22) | copy-start | bytes 772
  839.5 6.2 copy-start.6
  901.2 6.2 copy-start.6
  963.1 10.7 copy-start.9
  971.8 197.4 %reduce-scatter.13.cloned.1.call-start = ((), (), s32[]{:S(2)}) async-start(), calls=%async_computation.19 | async-start | bytes 9732096 | tf_op jit(solution)/shard_map/reduce_scatter | solution.py:288
  974.5 46.6 %copy-start.8 = (bf16[256,2048]{1,0:T(8,128)(2,1)S(1)}, bf16[256,2048]{1,0:T(8,128)(2,1)}, u32[]{:S(2)}) copy-start(bf16[256,2048]{1,0:T(8,128)(2,1)} %param.17) | copy-start | bytes 3145732
  974.5 46.6 %copy-start.14 = (f32[1,2048]{1,0:T(1,128)S(1)}, f32[1,2048]{1,0:T(1,128)}, u32[]{:S(2)}) copy-start(f32[1,2048]{1,0:T(1,128)} %copy-done.13) | copy-start | bytes 24580
  974.5 46.6 %copy-start.20 = (f32[256]{0:T(256)S(1)}, f32[256]{0:T(256)}, u32[]{:S(2)}) copy-start(f32[256]{0:T(256)} %copy-done.19) | copy-start | bytes 3076
  1019.9 6.6 copy-start.10
  1021.1 5.4 copy-start.12
  1034.7 1.6 copy-start.4
  1034.7 321.9 %reduce-scatter.15.cloned.1.call-start = ((), (), s32[]{:S(2)}) async-start(), calls=%async_computation.21 | async-start | bytes 8650752 | tf_op jit(solution)/shard_map/reduce_scatter | solution.py:288
  1051.9 465.9 %reduce-scatter.17.cloned.1.call-start = ((), (), s32[]{:S(2)}) async-start(), calls=%async_computation.23 | async-start | bytes 11796480 | tf_op jit(solution)/shard_map/reduce_scatter | solution.py:258
  1052.0 10.8 copy-start.27
  1052.0 10.8 copy-start.28
  1090.2 431.9 %copy-start.2 = (s32[166]{0:T(256)S(1)}, s32[166]{0:T(256)}, u32[]{:S(2)}) copy-start(s32[166]{0:T(256)} %param.20) | copy-start | bytes 1996
  1090.2 491.4 %all-gather.23.cloned.1.call-start = ((), (), s32[]{:S(2)}) async-start(), calls=%async_computation.20 | async-start | bytes 2654208 | tf_op jit(solution)/shard_map/all_gather | solution.py:289
  1169.2 412.3 %all-gather.25.cloned.1.call-start = ((), (), s32[]{:S(2)}) async-start(), calls=%async_computation.22 | async-start | bytes 2359296 | tf_op jit(solution)/shard_map/all_gather | solution.py:289
  1356.6 323.7 %all-gather.27.cloned.1.call-start = ((), (), s32[]{:S(2)}) async-start(), calls=%async_computation.24 | async-start | bytes 21233664 | tf_op jit(solution)/shard_map/all_gather | solution.py:260
  1525.0 9.3 copy-start.18
  1525.0 51.2 %copy-start.16 = (f32[2,2048]{1,0:T(2,128)S(1)}, f32[2,2048]{1,0:T(2,128)}, u32[]{:S(2)}) copy-start(f32[2,2048]{1,0:T(2,128)} %param.27) | copy-start | bytes 49156
  1525.1 51.2 %copy-start.21 = (f32[2,2048]{1,0:T(2,128)S(1)}, f32[2,2048]{1,0:T(2,128)}, u32[]{:S(2)}) copy-start(f32[2,2048]{1,0:T(2,128)} %param.28) | copy-start | bytes 49156
  1575.6 10.7 copy-start.17
  1599.6 89.7 %copy-start.24 = (pred[21]{0:T(512)(128)(4,1)S(1)}, pred[21]{0:T(512)(128)(4,1)}, u32[]{:S(2)}) copy-start(pred[21]{0:T(512)(128)(4,1)} %get-tuple-element.671) | copy-start | bytes 67
  1599.6 89.7 %copy-start.25 = (pred[21]{0:T(512)(128)(4,1)S(1)}, pred[21]{0:T(512)(128)(4,1)}, u32[]{:S(2)}) copy-start(pred[21]{0:T(512)(128)(4,1)} %broadcast_compare_fusion) | copy-start | bytes 67
Sparse Core Ops, SparseCore 0:
  9.9 114.7 all-gather.10
  134.5 48.3 all-gather.12
  184.8 93.1 all-gather.14
  279.9 219.8 all-gather.18
  502.1 52.5 all-gather.16
  556.5 54.3 all-gather.20
  648.2 71.2 reduce-scatter.8
  723.3 71.2 reduce-scatter.6
  971.9 35.7 reduce-scatter.10
  1034.8 134.3 reduce-scatter.12
  1171.5 185.0 reduce-scatter.14
  1358.8 158.9 reduce-scatter.16
  1519.7 29.8 all-gather.22
  1551.3 27.9 all-gather.24
  1581.6 98.6 all-gather.26
